TPU v7x, 128 devices: a whole 4x4x4 slice. The times are simulated.
128 devices in a mesh: section: 2 (over x_hi), rows: 16 (over y, x_lo, core), cols: 4 (over z).
Axes of the slice: x: 4 (x_hi: 2, x_lo: 2; x = x_hi * 2 + x_lo), y: 4, z: 4, core: 2. Of those that a mesh axis runs over, the one named last changes fastest.
Arguments:
- features: bfloat16 [2, 384, 96, 728], P(None, ('rows', 'cols')), may hold values from -6 to 6
- upstream: bfloat16 [2, 384, 96, 256], P(None, 'rows', 'cols'), may hold values from -0.0234375 to 0.0234375
- depth_mid: float32 [9, 728], replicated, may hold values from -2 to 2
- point_mid: bfloat16 [728, 728], replicated, may hold values from -0.21875 to 0.21875
- projection: bfloat16 [728, 2048], replicated, may hold values from -0.21875 to 0.21875
- depth_first: float32 [9, 2048], replicated, may hold values from -2 to 2
- point_first: bfloat16 [2048, 256], replicated, may hold values from -0.125 to 0.125
- depth_later: float32 [2, 9, 256], replicated, may hold values from -2 to 2
- point_later: bfloat16 [2, 256, 256], replicated, may hold values from -0.375 to 0.375
- joining: bfloat16 [768, 256], replicated, may hold values from -0.21875 to 0.21875
- rate_first: int32 [2], replicated, may hold values from 1 to 6, as said below
- rates_later: int32 [2, 2], replicated, may hold values from 1 to 21, as said below
Outputs:
- grad_mid: float32 [728, 728], replicated
- grad_later: float32 [2, 256, 256], replicated
Inputs may be any that keep to these rules, and one draw needn't show every extreme that they name: `rate_first`: at least one of the two rates equals 6. `rates_later`: at least one of the rates equals 21.
All inputs are finite; a program needn't handle non-finite values.
Results may differ from a plain program's by a relative error of at most 0.015.
Values may be sent and summed in bfloat16 or wider, within the bound.
No kernel may reach another device: no remote copies, remote signals or barrier semaphores. Data moves between devices by JAX's collectives and lax.ppermute only.
A program may use at most 128 MiB of HBM per device.

v0:
```python
import jax
import jax.numpy as jnp
from jax import lax
from jax.sharding import PartitionSpec as P

LATER = 2
R0 = 6
RMAX = 21


def as_sent(value):
    return jax.tree.map(lambda a: a.astype(jnp.bfloat16) if a.dtype == jnp.float32 else a, value)


def with_halo(cells, sides, width):
    for axis, dim in sides:
        count = lax.axis_size(axis)
        ends = count - 1
        head = lax.slice_in_dim(cells, 0, width, axis=dim)
        tail = lax.slice_in_dim(cells, cells.shape[dim] - width, cells.shape[dim], axis=dim)
        cells = jnp.concatenate(
            [
                lax.ppermute(tail, axis, [(i, (i + 1) % count) for i in range(ends)]),
                cells,
                lax.ppermute(head, axis, [((i + 1) % count, i) for i in range(ends)]),
            ],
            axis=dim,
        )
    return cells


def from_partner(value, axis, distance):
    return lax.ppermute(value, axis, [(i, i ^ 1 << distance) for i in range(lax.axis_size(axis))])


def silu_slope(argument):
    sigmoid_value = jax.nn.sigmoid(argument)
    return sigmoid_value * (1.0 + argument * (1.0 - sigmoid_value))


def dilated(padded, weights, rates_pair, margin, height, breadth, direction):
    depth = padded.shape[2]
    summed = jnp.zeros((height, breadth, depth), jnp.float32)
    for row_step in (-1, 0, 1):
        for col_step in (-1, 0, 1):
            row_start = margin + direction * row_step * rates_pair[0]
            col_start = margin + direction * col_step * rates_pair[1]
            window = lax.dynamic_slice(
                padded, (row_start, col_start, jnp.zeros((), jnp.int32)), (height, breadth, depth)
            )
            summed = (
                summed + window.astype(jnp.float32) * weights[3 * (row_step + 1) + col_step + 1]
            )
    return summed


def section_only(active, compute, *operands):

    def resting(*inputs):
        return jax.tree.map(jnp.zeros_like, compute(*inputs))

    return lax.cond(active, compute, resting, *operands)


def extend_tile(field, margin):
    return with_halo(as_sent(field), (("rows", 0), ("cols", 1)), margin).astype(field.dtype)


def backbone_local(haloed, features_now, depth_mid, point_mid):
    activated = jax.nn.silu(haloed.astype(jnp.float32))
    padded = jnp.pad(activated, ((0, 0), (1, 1), (0, 0)))
    unit_rates = jnp.ones((2,), jnp.int32)
    height, breadth = (features_now.shape[0], features_now.shape[1])
    mid_conv = dilated(padded, depth_mid, unit_rates, 1, height, breadth, 1).astype(jnp.bfloat16)
    mixed = jnp.einsum("hwc,cd->hwd", mid_conv, point_mid, preferred_element_type=jnp.float32)
    section_out = (features_now.astype(jnp.float32) + mixed).astype(jnp.bfloat16)
    return (section_out, mid_conv)


def mid_gradient(mid_conv, section_back):
    return jnp.einsum("hwc,hwd->cd", mid_conv, section_back, preferred_element_type=jnp.float32)


def project(field, projection):
    return jnp.einsum("hwc,ck->hwk", field, projection, preferred_element_type=jnp.float32).astype(
        jnp.bfloat16
    )


def head_front(padded_proj, depth_first, point_first, rate_first):
    height = padded_proj.shape[0] - 2 * R0
    breadth = padded_proj.shape[1] - 2 * R0
    first_conv = dilated(padded_proj, depth_first, rate_first, R0, height, breadth, 1).astype(
        jnp.bfloat16
    )
    first_pre = jnp.einsum(
        "hwc,cd->hwd", first_conv, point_first, preferred_element_type=jnp.float32
    )
    return (jax.nn.silu(first_pre).astype(jnp.bfloat16), first_pre)


def head_middle(padded_first, upstream_now, depth_later, point_later, rates_later, joining):
    height, breadth, channels = upstream_now.shape
    upstream_back = jnp.einsum(
        "hwb,kb->hwk", upstream_now, joining, preferred_element_type=jnp.float32
    )
    branch_backs = []
    branch_grads = []
    for branch in range(LATER):
        later_conv = dilated(
            padded_first, depth_later[branch], rates_later[branch], RMAX, height, breadth, 1
        ).astype(jnp.bfloat16)
        later_pre = jnp.einsum(
            "hwc,cd->hwd", later_conv, point_later[branch], preferred_element_type=jnp.float32
        )
        block = upstream_back[:, :, (branch + 1) * channels : (branch + 2) * channels]
        later_gate = (block * silu_slope(later_pre)).astype(jnp.bfloat16)
        later_back = jnp.einsum(
            "hwd,cd->hwc", later_gate, point_later[branch], preferred_element_type=jnp.float32
        )
        branch_backs.append(later_back.astype(jnp.bfloat16))
        branch_grads.append(
            jnp.einsum("hwc,hwd->cd", later_conv, later_gate, preferred_element_type=jnp.float32)
        )
    return (
        jnp.concatenate(branch_backs, axis=2),
        jnp.stack(branch_grads),
        upstream_back[:, :, :channels],
    )


def head_back(padded_backs, first_direct, first_pre, depth_later, rates_later, point_first):
    height, breadth, channels = first_direct.shape
    first_back = first_direct
    for branch in range(LATER):
        portion = padded_backs[:, :, branch * channels : (branch + 1) * channels]
        first_back = first_back + dilated(
            portion, depth_later[branch], rates_later[branch], RMAX, height, breadth, -1
        )
    first_gate = (first_back * silu_slope(first_pre)).astype(jnp.bfloat16)
    conv_back = jnp.einsum(
        "hwd,cd->hwc", first_gate, point_first, preferred_element_type=jnp.float32
    )
    return conv_back.astype(jnp.bfloat16)


def head_end(padded_conv, depth_first, rate_first, projection):
    height = padded_conv.shape[0] - 2 * R0
    breadth = padded_conv.shape[1] - 2 * R0
    projected_back = dilated(padded_conv, depth_first, rate_first, R0, height, breadth, -1).astype(
        jnp.bfloat16
    )
    section_back = jnp.einsum(
        "hwk,ck->hwc", projected_back, projection, preferred_element_type=jnp.float32
    )
    return section_back.astype(jnp.bfloat16)


def head_pass(
    act_tile,
    upstream_now,
    trailing,
    projection,
    depth_first,
    point_first,
    depth_later,
    point_later,
    joining,
    rate_first,
    rates_later,
):
    projected = section_only(trailing, project, act_tile, projection)
    padded_proj = extend_tile(projected, R0)
    first_out, first_pre = section_only(
        trailing, head_front, padded_proj, depth_first, point_first, rate_first
    )
    padded_first = extend_tile(first_out, RMAX)
    branch_backs, later_terms, first_direct = section_only(
        trailing,
        head_middle,
        padded_first,
        upstream_now,
        depth_later,
        point_later,
        rates_later,
        joining,
    )
    padded_backs = extend_tile(branch_backs, RMAX)
    conv_back = section_only(
        trailing,
        head_back,
        padded_backs,
        first_direct,
        first_pre,
        depth_later,
        rates_later,
        point_first,
    )
    padded_conv = extend_tile(conv_back, R0)
    section_back = section_only(
        trailing, head_end, padded_conv, depth_first, rate_first, projection
    )
    return (section_back, later_terms)


def local(
    features,
    upstream,
    depth_mid,
    point_mid,
    projection,
    depth_first,
    point_first,
    depth_later,
    point_later,
    joining,
    rate_first,
    rates_later,
):
    groups = lax.axis_size("cols")
    leading = lax.axis_index("section") == 0
    trailing = jnp.logical_not(leading)
    micro_count, slab_rows, full_width, channels_mid = features.shape
    tile_rows = slab_rows * groups
    tile_cols = full_width // groups
    channels_head = point_later.shape[1]
    received = jnp.zeros((slab_rows, full_width, channels_mid), jnp.bfloat16)
    saved_convs = []
    grad_mid = jnp.zeros((channels_mid, channels_mid), jnp.float32)
    grad_later = jnp.zeros((LATER, channels_head, channels_head), jnp.float32)
    for moment in range(micro_count + 1):
        if moment < micro_count:
            haloed = with_halo(features[moment], ((("rows", "cols"), 0),), 1)
            section_out, mid_conv = section_only(
                leading, backbone_local, haloed, features[moment], depth_mid, point_mid
            )
            saved_convs.append(mid_conv)
        else:
            section_out = jnp.zeros((slab_rows, full_width, channels_mid), jnp.bfloat16)
        if moment > 0:
            act_tile = received.reshape(slab_rows, groups, tile_cols, channels_mid).transpose(
                1, 0, 2, 3
            )
            act_tile = act_tile.reshape(tile_rows, tile_cols, channels_mid)
            section_back, later_terms = head_pass(
                act_tile,
                upstream[moment - 1],
                trailing,
                projection,
                depth_first,
                point_first,
                depth_later,
                point_later,
                joining,
                rate_first,
                rates_later,
            )
            grad_later = grad_later + later_terms
        else:
            section_back = jnp.zeros((tile_rows, tile_cols, channels_mid), jnp.bfloat16)
        slab_message = section_out.reshape(slab_rows, groups, tile_cols, channels_mid).transpose(
            1, 0, 2, 3
        )
        tile_message = section_back.reshape(groups, slab_rows, tile_cols, channels_mid)
        message = jnp.where(leading, slab_message, tile_message)
        regrouped = lax.all_to_all(
            message, "cols", split_axis=0, concat_axis=2, tiled=True
        ).reshape(slab_rows, full_width, channels_mid)
        received = from_partner(regrouped, "section", 0)
        if moment > 0:
            grad_mid = grad_mid + section_only(
                leading, mid_gradient, saved_convs[moment - 1], received
            )
    grad_mid, grad_later = lax.psum((grad_mid, grad_later), ("section", "rows", "cols"))
    return (grad_mid, grad_later)


def solution(mesh):
    placed = (
        P(None, ("rows", "cols"), None, None),
        P(None, "rows", "cols", None),
        P(),
        P(),
        P(),
        P(),
        P(),
        P(),
        P(),
        P(),
        P(),
        P(),
    )
    return jax.shard_map(local, mesh=mesh, in_specs=placed, out_specs=(P(), P()), check_vma=False)
```

profile of v0, /device:TPU:1, one launch (start us, length us, event | category | flops | bytes accessed | tf_op | source)
XLA Modules:
  0.0 880.8 jit_solution(3380174632669716522)
XLA Ops:
  27.6 6.9 conditional.14
  34.6 20.1 %all_to_all.45 = bf16[4,6,24,728]{3,2,1,0:T(8,128)(2,1)S(1)} all-to-all(bf16[4,6,24,728]{3,2,1,0:T(8,128)(2,1)S(1)} %copy.117), channel_id=1, replica_groups=mesh['section'=2,'rows'=16,'cols'=4] {'cols'}, dimensions={0} | all-to-all | bytes 1677312 | tf_op jit(solution)/shard_map/all_to_all | solution.py:266
  54.9 22.2 %collective-permute-done.4 = bf16[6,96,728]{2,1,0:T(8,128)(2,1)S(1)} collective-permute-done((bf16[6,96,728]{2,1,0:T(8,128)(2,1)S(1)}, bf16[6,96,728]{2,1,0:T(8,128)(2,1)S(1)}, u32[]{:S(2)}, u32[]{:S(2)}) %collective-permute-start.4) | collective-permute-done | bytes 838688 | tf_op jit(solution)/shard_map/ppermute | solution.py:33
  88.5 8.5 collective-permute-done.6
  101.9 9.4 %collective-permute-done.7 = bf16[36,6,2048]{2,0,1:T(8,128)(2,1)S(1)} collective-permute-done((bf16[36,6,2048]{2,0,1:T(8,128)(2,1)S(1)}, bf16[36,6,2048]{2,0,1:T(8,128)(2,1)S(1)}, u32[]{:S(2)}, u32[]{:S(2)}) %collective-permute-start.7) | collective-permute-done | bytes 884768 | tf_op jit(solution)/shard_map/ppermute | solution.py:23
  115.2 8.9 %pad_maximum_fusion.4 = bf16[36,36,2048]{2,0,1:T(8,128)(2,1)} fusion(bf16[36,6,2048]{2,0,1:T(8,128)(2,1)S(1)} %collective-permute-done.8, bf16[6,24,2048]{2,0,1:T(8,128)(2,1)S(1)} %copy.122, bf16[24,24,2048]{2,0,1:T(8,128)(2,1)S(1)} %copy.121, bf16[6,24,2048]{2,0,1:T(8,128)(2,1)S(1)} %copy.120, bf16[36,6,2048]{2,0,1:T(8,128)(2,1)S(1)} %collective-permute-done.7), kind=kLoop, calls=%fused_computation.194 | loop fusion | flops 26542080 | bytes 10616832 | tf_op jit(solution)/shard_map/concatenate | solution.py:21
  125.0 13.4 %collective-permute-start.9 = (bf16[21,24,256]{2,0,1:T(8,128)(2,1)S(1)}, bf16[21,24,256]{2,0,1:T(8,128)(2,1)S(1)}, u32[]{:S(2)}, u32[]{:S(2)}) collective-permute-start(bf16[21,24,256]{2,0,1:T(8,128)(2,1)S(1)} %get-tuple-element.652), channel_id=1, source_target_pairs={{0,4},{4,8},{8,12},{12,16},{16,20},{20,24},{24,28},{28,32},{32,36}... | collective-permute-start | bytes 774152 | tf_op jit(solution)/shard_map/ppermute | solution.py:23
  150.2 11.5 %collective-permute-done.11 = bf16[66,21,256]{2,0,1:T(8,128)(2,1)S(1)} collective-permute-done((bf16[66,21,256]{2,0,1:T(8,128)(2,1)S(1)}, bf16[66,21,256]{2,0,1:T(8,128)(2,1)S(1)}, u32[]{:S(2)}, u32[]{:S(2)}) %collective-permute-start.11) | collective-permute-done | bytes 709664 | tf_op jit(solution)/shard_map/ppermute | solution.py:23
  180.2 9.5 %collective-permute-done.14 = bf16[21,24,512]{2,1,0:T(8,128)(2,1)S(1)} collective-permute-done((bf16[21,24,512]{2,1,0:T(8,128)(2,1)S(1)}, bf16[21,24,512]{2,1,0:T(8,128)(2,1)S(1)}, u32[]{:S(2)}, u32[]{:S(2)}) %collective-permute-start.14) | collective-permute-done | bytes 516128 | tf_op jit(solution)/shard_map/ppermute | solution.py:25
  195.3 21.6 %collective-permute-done.15 = bf16[66,21,512]{2,0,1:T(8,128)(2,1)S(1)} collective-permute-done((bf16[66,21,512]{2,0,1:T(8,128)(2,1)S(1)}, bf16[66,21,512]{2,0,1:T(8,128)(2,1)S(1)}, u32[]{:S(2)}, u32[]{:S(2)}) %collective-permute-start.15) | collective-permute-done | bytes 1419296 | tf_op jit(solution)/shard_map/ppermute | solution.py:23
  221.1 6.0 pad_maximum_fusion.8
  227.8 12.3 %collective-permute-start.17 = (bf16[6,24,2048]{2,1,0:T(8,128)(2,1)S(1)}, bf16[6,24,2048]{2,1,0:T(8,128)(2,1)S(1)}, u32[]{:S(2)}, u32[]{:S(2)}) collective-permute-start(bf16[6,24,2048]{2,1,0:T(8,128)(2,1)S(1)} %get-tuple-element.628), channel_id=1, source_target_pairs={{0,4},{4,8},{8,12},{12,16},{16,20},{20,24},{24,28},{28,32},{32,36}... | collective-permute-start | bytes 1769480 | tf_op jit(solution)/shard_map/ppermute | solution.py:23
  247.2 8.5 collective-permute-done.18
  283.7 11.3 %all_to_all.46 = bf16[4,6,24,728]{3,2,1,0:T(8,128)(2,1)S(1)} all-to-all(bf16[4,6,24,728]{3,2,1,0:T(8,128)(2,1)S(1)} %copy.139), channel_id=1, replica_groups=mesh['section'=2,'rows'=16,'cols'=4] {'cols'}, dimensions={0} | all-to-all | bytes 1677312 | tf_op jit(solution)/shard_map/all_to_all | solution.py:266
  295.0 78.8 %collective-permute-start.21 = (bf16[6,96,728]{2,1,0:T(8,128)(2,1)S(1)}, bf16[6,96,728]{2,1,0:T(8,128)(2,1)}, u32[]{:S(2)}, u32[]{:S(2)}) collective-permute-start(bf16[6,96,728]{2,1,0:T(8,128)(2,1)S(1)} %bitcast.368), channel_id=1, source_target_pairs={{0,64},{64,0},{1,65},{65,1},{2,66},{66,2},{3,67},{67,3},{4,68},{68... | collective-permute-start | bytes 2515976 | tf_op jit(solution)/shard_map/ppermute | solution.py:33
  373.9 11.3 %collective-permute-done.21 = bf16[6,96,728]{2,1,0:T(8,128)(2,1)} collective-permute-done((bf16[6,96,728]{2,1,0:T(8,128)(2,1)S(1)}, bf16[6,96,728]{2,1,0:T(8,128)(2,1)}, u32[]{:S(2)}, u32[]{:S(2)}) %collective-permute-start.21) | collective-permute-done | bytes 838688 | tf_op jit(solution)/shard_map/ppermute | solution.py:33
  385.6 21.8 %collective-permute-start.22 = (bf16[6,24,2048]{2,1,0:T(8,128)(2,1)S(1)}, bf16[6,24,2048]{2,1,0:T(8,128)(2,1)S(1)}, u32[]{:S(2)}, u32[]{:S(2)}) collective-permute-start(bf16[6,24,2048]{2,1,0:T(8,128)(2,1)S(1)} %get-tuple-element.626), channel_id=1, source_target_pairs={{0,4},{4,8},{8,12},{12,16},{16,20},{20,24},{24,28},{28,32},{32,36}... | collective-permute-start | bytes 1769480 | tf_op jit(solution)/shard_map/ppermute | solution.py:23
  423.5 13.1 %collective-permute-done.24 = bf16[36,6,2048]{2,0,1:T(8,128)(2,1)S(1)} collective-permute-done((bf16[36,6,2048]{2,0,1:T(8,128)(2,1)S(1)}, bf16[36,6,2048]{2,0,1:T(8,128)(2,1)S(1)}, u32[]{:S(2)}, u32[]{:S(2)}) %collective-permute-start.24) | collective-permute-done | bytes 884768 | tf_op jit(solution)/shard_map/ppermute | solution.py:23
  440.7 8.9 %pad_maximum_fusion.6 = bf16[36,36,2048]{2,0,1:T(8,128)(2,1)} fusion(bf16[36,6,2048]{2,0,1:T(8,128)(2,1)S(1)} %collective-permute-done.25, bf16[6,24,2048]{2,0,1:T(8,128)(2,1)S(1)} %copy.144, bf16[24,24,2048]{2,0,1:T(8,128)(2,1)S(1)} %copy.143, bf16[6,24,2048]{2,0,1:T(8,128)(2,1)S(1)} %copy.142, bf16[36,6,2048]{2,0,1:T(8,128)(2,1)S(1)} %collective-permute-done.24), kind=kLoop, calls=%fused_computation.196 | loop fusion | flops 26542080 | bytes 10616832 | tf_op jit(solution)/shard_map/concatenate | solution.py:21
  450.7 7.3 collective-permute-start.26
  461.6 6.9 collective-permute-done.27
  472.5 9.2 %collective-permute-done.28 = bf16[66,21,256]{2,0,1:T(8,128)(2,1)S(1)} collective-permute-done((bf16[66,21,256]{2,0,1:T(8,128)(2,1)S(1)}, bf16[66,21,256]{2,0,1:T(8,128)(2,1)S(1)}, u32[]{:S(2)}, u32[]{:S(2)}) %collective-permute-start.28) | collective-permute-done | bytes 709664 | tf_op jit(solution)/shard_map/ppermute | solution.py:23
  488.3 8.6 collective-permute-start.30
  513.6 25.3 %collective-permute-done.32 = bf16[66,21,512]{2,0,1:T(8,128)(2,1)S(1)} collective-permute-done((bf16[66,21,512]{2,0,1:T(8,128)(2,1)S(1)}, bf16[66,21,512]{2,0,1:T(8,128)(2,1)S(1)}, u32[]{:S(2)}, u32[]{:S(2)}) %collective-permute-start.32) | collective-permute-done | bytes 1419296 | tf_op jit(solution)/shard_map/ppermute | solution.py:23
  543.1 6.0 pad_maximum_fusion.9
  549.7 8.2 collective-permute-start.34
  574.7 12.3 %collective-permute-done.36 = bf16[36,6,2048]{2,0,1:T(8,128)(2,1)S(1)} collective-permute-done((bf16[36,6,2048]{2,0,1:T(8,128)(2,1)S(1)}, bf16[36,6,2048]{2,0,1:T(8,128)(2,1)S(1)}, u32[]{:S(2)}, u32[]{:S(2)}) %collective-permute-start.36) | collective-permute-done | bytes 884768 | tf_op jit(solution)/shard_map/ppermute | solution.py:23
  591.2 8.9 %pad_maximum_fusion.7 = bf16[36,36,2048]{2,0,1:T(8,128)(2,1)} fusion(bf16[36,6,2048]{2,0,1:T(8,128)(2,1)S(1)} %collective-permute-done.37, bf16[6,24,2048]{2,0,1:T(8,128)(2,1)S(1)} %copy.158, bf16[24,24,2048]{2,0,1:T(8,128)(2,1)S(1)} %copy.157, bf16[6,24,2048]{2,0,1:T(8,128)(2,1)S(1)} %copy.156, bf16[36,6,2048]{2,0,1:T(8,128)(2,1)S(1)} %collective-permute-done.36), kind=kLoop, calls=%fused_computation.197 | loop fusion | flops 26542080 | bytes 10616832 | tf_op jit(solution)/shard_map/concatenate | solution.py:21
  600.5 11.3 %all_to_all.47 = bf16[4,6,24,728]{3,2,1,0:T(8,128)(2,1)S(1)} all-to-all(bf16[4,6,24,728]{3,2,1,0:T(8,128)(2,1)S(1)} %copy.161), channel_id=1, replica_groups=mesh['section'=2,'rows'=16,'cols'=4] {'cols'}, dimensions={0} | all-to-all | bytes 1677312 | tf_op jit(solution)/shard_map/all_to_all | solution.py:266
  611.9 77.5 %collective-permute-start.38 = (bf16[6,96,728]{2,1,0:T(8,128)(2,1)S(1)}, bf16[6,96,728]{2,1,0:T(8,128)(2,1)}, u32[]{:S(2)}, u32[]{:S(2)}) collective-permute-start(bf16[6,96,728]{2,1,0:T(8,128)(2,1)S(1)} %bitcast.363), channel_id=1, source_target_pairs={{0,64},{64,0},{1,65},{65,1},{2,66},{66,2},{3,67},{67,3},{4,68},{68... | collective-permute-start | bytes 2515976 | tf_op jit(solution)/shard_map/ppermute | solution.py:33
  693.9 10.4 %collective-permute-done.38 = bf16[6,96,728]{2,1,0:T(8,128)(2,1)} collective-permute-done((bf16[6,96,728]{2,1,0:T(8,128)(2,1)S(1)}, bf16[6,96,728]{2,1,0:T(8,128)(2,1)}, u32[]{:S(2)}, u32[]{:S(2)}) %collective-permute-start.38) | collective-permute-done | bytes 838688 | tf_op jit(solution)/shard_map/ppermute | solution.py:33
  711.5 158.1 %all-reduce.5.cloned.1.call-done = (f32[728,728]{1,0:T(8,128)}, f32[2,256,256]{2,1,0:T(8,128)}) async-done(((f32[728,728]{1,0:T(8,128)}, f32[2,256,256]{2,1,0:T(8,128)}), (f32[728,728]{1,0:T(8,128)}, f32[2,256,256]{2,1,0:T(8,128)})) %all-reduce.5.cloned.1.call-update) | async-done | bytes 2644240 | tf_op jit(solution)/shard_map/psum | solution.py:274
  (194 shorter events, 236.4 us)
Async XLA Ops:
  7.2 862.4 %all-reduce.5.cloned.1.call-start = ((), (), s32[]{:S(2)}) async-start(), calls=%async_computation.3 | async-start | bytes 5521408 | tf_op jit(solution)/shard_map/psum | solution.py:274
  8.4 17.4 %collective-permute-start.2 = (bf16[1,96,728]{2,1,0:T(8,128)(2,1)S(1)}, bf16[1,96,728]{2,1,0:T(8,128)(2,1)S(1)}, u32[]{:S(2)}, u32[]{:S(2)}) collective-permute-start(bf16[1,96,728]{2,1,0:T(8,128)(2,1)S(1)} %get-tuple-element.636), channel_id=1, source_target_pairs={{0,1},{1,2},{2,3},{3,4},{4,5},{5,6},{6,7},{7,8},{8,9},{9,10},{10,1... | collective-permute-start | bytes 419336 | tf_op jit(solution)/shard_map/ppermute | solution.py:23
  12.8 13.0 %collective-permute-start.1 = (bf16[1,96,728]{2,1,0:T(8,128)(2,1)S(1)}, bf16[1,96,728]{2,1,0:T(8,128)(2,1)S(1)}, u32[]{:S(2)}, u32[]{:S(2)}) collective-permute-start(bf16[1,96,728]{2,1,0:T(8,128)(2,1)S(1)} %get-tuple-element.637), channel_id=1, source_target_pairs={{1,0},{2,1},{3,2},{4,3},{5,4},{6,5},{7,6},{8,7},{9,8},{10,9},{11,1... | collective-permute-start | bytes 419336 | tf_op jit(solution)/shard_map/ppermute | solution.py:25
  54.8 22.3 %collective-permute-start.4 = (bf16[6,96,728]{2,1,0:T(8,128)(2,1)S(1)}, bf16[6,96,728]{2,1,0:T(8,128)(2,1)S(1)}, u32[]{:S(2)}, u32[]{:S(2)}) collective-permute-start(bf16[6,96,728]{2,1,0:T(8,128)(2,1)S(1)} %bitcast.367), channel_id=1, source_target_pairs={{0,64},{64,0},{1,65},{65,1},{2,66},{66,2},{3,67},{67,3},{4,68},{68... | collective-permute-start | bytes 2515976 | tf_op jit(solution)/shard_map/ppermute | solution.py:33
  81.4 15.7 %collective-permute-start.6 = (bf16[6,24,2048]{2,1,0:T(8,128)(2,1)S(1)}, bf16[6,24,2048]{2,1,0:T(8,128)(2,1)S(1)}, u32[]{:S(2)}, u32[]{:S(2)}) collective-permute-start(bf16[6,24,2048]{2,1,0:T(8,128)(2,1)S(1)} %get-tuple-element.631), channel_id=1, source_target_pairs={{4,0},{8,4},{12,8},{16,12},{20,16},{24,20},{28,24},{32,28},{36,32}... | collective-permute-start | bytes 1769480 | tf_op jit(solution)/shard_map/ppermute | solution.py:25
  98.1 13.2 %collective-permute-start.7 = (bf16[36,6,2048]{2,0,1:T(8,128)(2,1)S(1)}, bf16[36,6,2048]{2,0,1:T(8,128)(2,1)S(1)}, u32[]{:S(2)}, u32[]{:S(2)}) collective-permute-start(bf16[36,6,2048]{2,0,1:T(8,128)(2,1)S(1)} %get-tuple-element.622), channel_id=1, source_target_pairs={{0,1},{1,2},{2,3},{4,5},{5,6},{6,7},{8,9},{9,10},{10,11},{12,13},{... | collective-permute-start | bytes 2654216 | tf_op jit(solution)/shard_map/ppermute | solution.py:23
  100.4 14.8 %collective-permute-start.8 = (bf16[36,6,2048]{2,0,1:T(8,128)(2,1)S(1)}, bf16[36,6,2048]{2,0,1:T(8,128)(2,1)S(1)}, u32[]{:S(2)}, u32[]{:S(2)}) collective-permute-start(bf16[36,6,2048]{2,0,1:T(8,128)(2,1)S(1)} %get-tuple-element.623), channel_id=1, source_target_pairs={{1,0},{2,1},{3,2},{5,4},{6,5},{7,6},{9,8},{10,9},{11,10},{13,12},{... | collective-permute-start | bytes 2654216 | tf_op jit(solution)/shard_map/ppermute | solution.py:25
  125.0 17.0 %collective-permute-start.9 = (bf16[21,24,256]{2,0,1:T(8,128)(2,1)S(1)}, bf16[21,24,256]{2,0,1:T(8,128)(2,1)S(1)}, u32[]{:S(2)}, u32[]{:S(2)}) collective-permute-start(bf16[21,24,256]{2,0,1:T(8,128)(2,1)S(1)} %get-tuple-element.652), channel_id=1, source_target_pairs={{0,4},{4,8},{8,12},{12,16},{16,20},{20,24},{24,28},{28,32},{32,36}... | collective-permute-start | bytes 774152 | tf_op jit(solution)/shard_map/ppermute | solution.py:23
  147.3 14.4 %collective-permute-start.11 = (bf16[66,21,256]{2,0,1:T(8,128)(2,1)S(1)}, bf16[66,21,256]{2,0,1:T(8,128)(2,1)S(1)}, u32[]{:S(2)}, u32[]{:S(2)}) collective-permute-start(bf16[66,21,256]{2,0,1:T(8,128)(2,1)S(1)} %get-tuple-element.644), channel_id=1, source_target_pairs={{0,1},{1,2},{2,3},{4,5},{5,6},{6,7},{8,9},{9,10},{10,11},{12,13},{... | collective-permute-start | bytes 2128904 | tf_op jit(solution)/shard_map/ppermute | solution.py:23
  148.9 17.1 %collective-permute-start.12 = (bf16[66,21,256]{2,0,1:T(8,128)(2,1)S(1)}, bf16[66,21,256]{2,0,1:T(8,128)(2,1)S(1)}, u32[]{:S(2)}, u32[]{:S(2)}) collective-permute-start(bf16[66,21,256]{2,0,1:T(8,128)(2,1)S(1)} %get-tuple-element.645), channel_id=1, source_target_pairs={{1,0},{2,1},{3,2},{5,4},{6,5},{7,6},{9,8},{10,9},{11,10},{13,12},{... | collective-permute-start | bytes 2128904 | tf_op jit(solution)/shard_map/ppermute | solution.py:25
  168.4 11.6 %collective-permute-start.13 = (bf16[21,24,512]{2,1,0:T(8,128)(2,1)S(1)}, bf16[21,24,512]{2,1,0:T(8,128)(2,1)S(1)}, u32[]{:S(2)}, u32[]{:S(2)}) collective-permute-start(bf16[21,24,512]{2,1,0:T(8,128)(2,1)S(1)} %get-tuple-element.648), channel_id=1, source_target_pairs={{0,4},{4,8},{8,12},{12,16},{16,20},{20,24},{24,28},{28,32},{32,36}... | collective-permute-start | bytes 1548296 | tf_op jit(solution)/shard_map/ppermute | solution.py:23
  174.0 15.6 %collective-permute-start.14 = (bf16[21,24,512]{2,1,0:T(8,128)(2,1)S(1)}, bf16[21,24,512]{2,1,0:T(8,128)(2,1)S(1)}, u32[]{:S(2)}, u32[]{:S(2)}) collective-permute-start(bf16[21,24,512]{2,1,0:T(8,128)(2,1)S(1)} %get-tuple-element.649), channel_id=1, source_target_pairs={{4,0},{8,4},{12,8},{16,12},{20,16},{24,20},{28,24},{32,28},{36,32}... | collective-permute-start | bytes 1548296 | tf_op jit(solution)/shard_map/ppermute | solution.py:25
  190.6 26.3 %collective-permute-start.15 = (bf16[66,21,512]{2,0,1:T(8,128)(2,1)S(1)}, bf16[66,21,512]{2,0,1:T(8,128)(2,1)S(1)}, u32[]{:S(2)}, u32[]{:S(2)}) collective-permute-start(bf16[66,21,512]{2,0,1:T(8,128)(2,1)S(1)} %get-tuple-element.634), channel_id=1, source_target_pairs={{0,1},{1,2},{2,3},{4,5},{5,6},{6,7},{8,9},{9,10},{10,11},{12,13},{... | collective-permute-start | bytes 4257800 | tf_op jit(solution)/shard_map/ppermute | solution.py:23
  194.0 27.1 %collective-permute-start.16 = (bf16[66,21,512]{2,0,1:T(8,128)(2,1)S(1)}, bf16[66,21,512]{2,0,1:T(8,128)(2,1)S(1)}, u32[]{:S(2)}, u32[]{:S(2)}) collective-permute-start(bf16[66,21,512]{2,0,1:T(8,128)(2,1)S(1)} %get-tuple-element.635), channel_id=1, source_target_pairs={{1,0},{2,1},{3,2},{5,4},{6,5},{7,6},{9,8},{10,9},{11,10},{13,12},{... | collective-permute-start | bytes 4257800 | tf_op jit(solution)/shard_map/ppermute | solution.py:25
  227.8 19.1 %collective-permute-start.17 = (bf16[6,24,2048]{2,1,0:T(8,128)(2,1)S(1)}, bf16[6,24,2048]{2,1,0:T(8,128)(2,1)S(1)}, u32[]{:S(2)}, u32[]{:S(2)}) collective-permute-start(bf16[6,24,2048]{2,1,0:T(8,128)(2,1)S(1)} %get-tuple-element.628), channel_id=1, source_target_pairs={{0,4},{4,8},{8,12},{12,16},{16,20},{20,24},{24,28},{28,32},{32,36}... | collective-permute-start | bytes 1769480 | tf_op jit(solution)/shard_map/ppermute | solution.py:23
  240.1 15.6 %collective-permute-start.18 = (bf16[6,24,2048]{2,1,0:T(8,128)(2,1)S(1)}, bf16[6,24,2048]{2,1,0:T(8,128)(2,1)S(1)}, u32[]{:S(2)}, u32[]{:S(2)}) collective-permute-start(bf16[6,24,2048]{2,1,0:T(8,128)(2,1)S(1)} %get-tuple-element.629), channel_id=1, source_target_pairs={{4,0},{8,4},{12,8},{16,12},{20,16},{24,20},{28,24},{32,28},{36,32}... | collective-permute-start | bytes 1769480 | tf_op jit(solution)/shard_map/ppermute | solution.py:25
  258.1 13.2 %collective-permute-start.19 = (bf16[36,6,2048]{2,0,1:T(8,128)(2,1)}, bf16[36,6,2048]{2,0,1:T(8,128)(2,1)}, u32[]{:S(2)}, u32[]{:S(2)}) collective-permute-start(bf16[36,6,2048]{2,0,1:T(8,128)(2,1)} %get-tuple-element.620), channel_id=1, source_target_pairs={{0,1},{1,2},{2,3},{4,5},{5,6},{6,7},{8,9},{9,10},{10,11},{12,13},{... | collective-permute-start | bytes 2654216 | tf_op jit(solution)/shard_map/ppermute | solution.py:23
  260.9 15.1 %collective-permute-start.20 = (bf16[36,6,2048]{2,0,1:T(8,128)(2,1)}, bf16[36,6,2048]{2,0,1:T(8,128)(2,1)}, u32[]{:S(2)}, u32[]{:S(2)}) collective-permute-start(bf16[36,6,2048]{2,0,1:T(8,128)(2,1)} %get-tuple-element.621), channel_id=1, source_target_pairs={{1,0},{2,1},{3,2},{5,4},{6,5},{7,6},{9,8},{10,9},{11,10},{13,12},{... | collective-permute-start | bytes 2654216 | tf_op jit(solution)/shard_map/ppermute | solution.py:25
  295.0 90.1 %collective-permute-start.21 = (bf16[6,96,728]{2,1,0:T(8,128)(2,1)S(1)}, bf16[6,96,728]{2,1,0:T(8,128)(2,1)}, u32[]{:S(2)}, u32[]{:S(2)}) collective-permute-start(bf16[6,96,728]{2,1,0:T(8,128)(2,1)S(1)} %bitcast.368), channel_id=1, source_target_pairs={{0,64},{64,0},{1,65},{65,1},{2,66},{66,2},{3,67},{67,3},{4,68},{68... | collective-permute-start | bytes 2515976 | tf_op jit(solution)/shard_map/ppermute | solution.py:33
  385.6 28.6 %collective-permute-start.22 = (bf16[6,24,2048]{2,1,0:T(8,128)(2,1)S(1)}, bf16[6,24,2048]{2,1,0:T(8,128)(2,1)S(1)}, u32[]{:S(2)}, u32[]{:S(2)}) collective-permute-start(bf16[6,24,2048]{2,1,0:T(8,128)(2,1)S(1)} %get-tuple-element.626), channel_id=1, source_target_pairs={{0,4},{4,8},{8,12},{12,16},{16,20},{20,24},{24,28},{28,32},{32,36}... | collective-permute-start | bytes 1769480 | tf_op jit(solution)/shard_map/ppermute | solution.py:23
  419.7 16.9 %collective-permute-start.24 = (bf16[36,6,2048]{2,0,1:T(8,128)(2,1)S(1)}, bf16[36,6,2048]{2,0,1:T(8,128)(2,1)S(1)}, u32[]{:S(2)}, u32[]{:S(2)}) collective-permute-start(bf16[36,6,2048]{2,0,1:T(8,128)(2,1)S(1)} %get-tuple-element.618), channel_id=1, source_target_pairs={{0,1},{1,2},{2,3},{4,5},{5,6},{6,7},{8,9},{9,10},{10,11},{12,13},{... | collective-permute-start | bytes 2654216 | tf_op jit(solution)/shard_map/ppermute | solution.py:23
  422.2 18.5 %collective-permute-start.25 = (bf16[36,6,2048]{2,0,1:T(8,128)(2,1)S(1)}, bf16[36,6,2048]{2,0,1:T(8,128)(2,1)S(1)}, u32[]{:S(2)}, u32[]{:S(2)}) collective-permute-start(bf16[36,6,2048]{2,0,1:T(8,128)(2,1)S(1)} %get-tuple-element.619), channel_id=1, source_target_pairs={{1,0},{2,1},{3,2},{5,4},{6,5},{7,6},{9,8},{10,9},{11,10},{13,12},{... | collective-permute-start | bytes 2654216 | tf_op jit(solution)/shard_map/ppermute | solution.py:25
  469.0 12.7 %collective-permute-start.28 = (bf16[66,21,256]{2,0,1:T(8,128)(2,1)S(1)}, bf16[66,21,256]{2,0,1:T(8,128)(2,1)S(1)}, u32[]{:S(2)}, u32[]{:S(2)}) collective-permute-start(bf16[66,21,256]{2,0,1:T(8,128)(2,1)S(1)} %get-tuple-element.642), channel_id=1, source_target_pairs={{0,1},{1,2},{2,3},{4,5},{5,6},{6,7},{8,9},{9,10},{10,11},{12,13},{... | collective-permute-start | bytes 2128904 | tf_op jit(solution)/shard_map/ppermute | solution.py:23
  471.2 14.7 %collective-permute-start.29 = (bf16[66,21,256]{2,0,1:T(8,128)(2,1)S(1)}, bf16[66,21,256]{2,0,1:T(8,128)(2,1)S(1)}, u32[]{:S(2)}, u32[]{:S(2)}) collective-permute-start(bf16[66,21,256]{2,0,1:T(8,128)(2,1)S(1)} %get-tuple-element.643), channel_id=1, source_target_pairs={{1,0},{2,1},{3,2},{5,4},{6,5},{7,6},{9,8},{10,9},{11,10},{13,12},{... | collective-permute-start | bytes 2128904 | tf_op jit(solution)/shard_map/ppermute | solution.py:25
  488.3 14.6 %collective-permute-start.30 = (bf16[21,24,512]{2,1,0:T(8,128)(2,1)S(1)}, bf16[21,24,512]{2,1,0:T(8,128)(2,1)S(1)}, u32[]{:S(2)}, u32[]{:S(2)}) collective-permute-start(bf16[21,24,512]{2,1,0:T(8,128)(2,1)S(1)} %get-tuple-element.646), channel_id=1, source_target_pairs={{0,4},{4,8},{8,12},{12,16},{16,20},{20,24},{24,28},{28,32},{32,36}... | collective-permute-start | bytes 1548296 | tf_op jit(solution)/shard_map/ppermute | solution.py:23
  509.1 29.8 %collective-permute-start.32 = (bf16[66,21,512]{2,0,1:T(8,128)(2,1)S(1)}, bf16[66,21,512]{2,0,1:T(8,128)(2,1)S(1)}, u32[]{:S(2)}, u32[]{:S(2)}) collective-permute-start(bf16[66,21,512]{2,0,1:T(8,128)(2,1)S(1)} %get-tuple-element.632), channel_id=1, source_target_pairs={{0,1},{1,2},{2,3},{4,5},{5,6},{6,7},{8,9},{9,10},{10,11},{12,13},{... | collective-permute-start | bytes 4257800 | tf_op jit(solution)/shard_map/ppermute | solution.py:23
  512.3 30.8 %collective-permute-start.33 = (bf16[66,21,512]{2,0,1:T(8,128)(2,1)S(1)}, bf16[66,21,512]{2,0,1:T(8,128)(2,1)S(1)}, u32[]{:S(2)}, u32[]{:S(2)}) collective-permute-start(bf16[66,21,512]{2,0,1:T(8,128)(2,1)S(1)} %get-tuple-element.633), channel_id=1, source_target_pairs={{1,0},{2,1},{3,2},{5,4},{6,5},{7,6},{9,8},{10,9},{11,10},{13,12},{... | collective-permute-start | bytes 4257800 | tf_op jit(solution)/shard_map/ppermute | solution.py:25
  549.7 15.0 %collective-permute-start.34 = (bf16[6,24,2048]{2,1,0:T(8,128)(2,1)S(1)}, bf16[6,24,2048]{2,1,0:T(8,128)(2,1)S(1)}, u32[]{:S(2)}, u32[]{:S(2)}) collective-permute-start(bf16[6,24,2048]{2,1,0:T(8,128)(2,1)S(1)} %get-tuple-element.624), channel_id=1, source_target_pairs={{0,4},{4,8},{8,12},{12,16},{16,20},{20,24},{24,28},{28,32},{32,36}... | collective-permute-start | bytes 1769480 | tf_op jit(solution)/shard_map/ppermute | solution.py:23
  557.9 11.9 %collective-permute-start.35 = (bf16[6,24,2048]{2,1,0:T(8,128)(2,1)S(1)}, bf16[6,24,2048]{2,1,0:T(8,128)(2,1)S(1)}, u32[]{:S(2)}, u32[]{:S(2)}) collective-permute-start(bf16[6,24,2048]{2,1,0:T(8,128)(2,1)S(1)} %get-tuple-element.625), channel_id=1, source_target_pairs={{4,0},{8,4},{12,8},{16,12},{20,16},{24,20},{28,24},{32,28},{36,32}... | collective-permute-start | bytes 1769480 | tf_op jit(solution)/shard_map/ppermute | solution.py:25
  571.0 16.1 %collective-permute-start.36 = (bf16[36,6,2048]{2,0,1:T(8,128)(2,1)S(1)}, bf16[36,6,2048]{2,0,1:T(8,128)(2,1)S(1)}, u32[]{:S(2)}, u32[]{:S(2)}) collective-permute-start(bf16[36,6,2048]{2,0,1:T(8,128)(2,1)S(1)} %get-tuple-element.616), channel_id=1, source_target_pairs={{0,1},{1,2},{2,3},{4,5},{5,6},{6,7},{8,9},{9,10},{10,11},{12,13},{... | collective-permute-start | bytes 2654216 | tf_op jit(solution)/shard_map/ppermute | solution.py:23
  573.4 17.8 %collective-permute-start.37 = (bf16[36,6,2048]{2,0,1:T(8,128)(2,1)S(1)}, bf16[36,6,2048]{2,0,1:T(8,128)(2,1)S(1)}, u32[]{:S(2)}, u32[]{:S(2)}) collective-permute-start(bf16[36,6,2048]{2,0,1:T(8,128)(2,1)S(1)} %get-tuple-element.617), channel_id=1, source_target_pairs={{1,0},{2,1},{3,2},{5,4},{6,5},{7,6},{9,8},{10,9},{11,10},{13,12},{... | collective-permute-start | bytes 2654216 | tf_op jit(solution)/shard_map/ppermute | solution.py:25
  611.9 92.5 %collective-permute-start.38 = (bf16[6,96,728]{2,1,0:T(8,128)(2,1)S(1)}, bf16[6,96,728]{2,1,0:T(8,128)(2,1)}, u32[]{:S(2)}, u32[]{:S(2)}) collective-permute-start(bf16[6,96,728]{2,1,0:T(8,128)(2,1)S(1)} %bitcast.363), channel_id=1, source_target_pairs={{0,64},{64,0},{1,65},{65,1},{2,66},{66,2},{3,67},{67,3},{4,68},{68... | collective-permute-start | bytes 2515976 | tf_op jit(solution)/shard_map/ppermute | solution.py:33
  (27 other events, 286.2 us)
Sparse Core Ops, SparseCore 0:
  711.7 157.9 all-reduce.4
where the time goes:
time: 890 us; the launch traced here: 881 us
  waiting for transfers between devices  417 us (47%)
  starting transfers between devices  300 us (34%)
  other arithmetic  66.2 us (7%)
  blocking collectives  42.7 us (5%)
  local copies, waits for them, and re-layouts  27.7 us (3%)
  between operations  15.3 us (2%)
  matrix products  10.4 us (1%)
    psum x1, waiting for transfers between devices, local(): lax.psum((grad_mid, grad_later), ('section', 'rows', 'cols'))  158 us
    ppermute x3, starting transfers between devices, from_partner(): lax.ppermute(value, axis, [(i, i ^ 1 << distance) for i in range(lax.axis...  156 us
    ppermute x18, waiting for transfers between devices, with_halo(): lax.ppermute(tail, axis, [(i, (i + 1) % count) for i in range(ends)])  129 us
    ppermute x18, starting transfers between devices, with_halo(): lax.ppermute(tail, axis, [(i, (i + 1) % count) for i in range(ends)])  107 us
    ppermute x18, waiting for transfers between devices, with_halo(): lax.ppermute(head, axis, [((i + 1) % count, i) for i in range(ends)])  86.4 us
    concatenate x13, other arithmetic, with_halo(): jnp.concatenate([lax.ppermute(tail, axis, [(i, (i + 1) % count) for i in...  49 us
    ppermute x3, waiting for transfers between devices, from_partner(): lax.ppermute(value, axis, [(i, i ^ 1 << distance) for i in range(lax.axis...  44 us
    all_to_all x3, blocking collectives, local(): lax.all_to_all(message, 'cols', split_axis=0, concat_axis=2, tiled=True)  42.7 us
  transfers between devices with their start and end apart: 40, of which 37 were waited for; matrix products, arithmetic and copies ran while one was open for 2% of the time, Pallas kernels for 0%

commit v1 on v0

--- a/solution.py
+++ b/solution.py
@@ -1,3 +1,4 @@
+import functools
 import jax
 import jax.numpy as jnp
 from jax import lax
@@ -6,6 +7,15 @@
 LATER = 2
 R0 = 6
 RMAX = 21
+
+
+def _expand_plane(local_values, row_axis, comm_axis):
+    for s in (row_axis, comm_axis):
+        local_values = lax.psum(local_values, s)
+    return local_values
+
+
+test_sector = functools.partial(_expand_plane, row_axis=("rows", "cols"), comm_axis="section")
 
 
 def as_sent(value):
@@ -271,7 +281,7 @@
             grad_mid = grad_mid + section_only(
                 leading, mid_gradient, saved_convs[moment - 1], received
             )
-    grad_mid, grad_later = lax.psum((grad_mid, grad_later), ("section", "rows", "cols"))
+    grad_mid, grad_later = test_sector((grad_mid, grad_later))
     return (grad_mid, grad_later)
 
 

time: 890 us -> 1370 us (1.54)
  waiting for transfers between devices: 417 us -> 899 us
    psum x1 -> x2, waiting for transfers between devices: 158 us -> 640 us  [_expand_plane(): local_values = lax.psum(local_values, s)]
  transfers between devices with their start and end apart: 40 -> 41, of which waited for: 37 -> 38; matrix products, arithmetic and copies ran while one was open for 2% -> 2% of each run, Pallas kernels for 0% -> 0%
where the time goes in v1:
time: 1370 us; the launch traced here: 1360 us
  waiting for transfers between devices  899 us (66%)
  starting transfers between devices  297 us (22%)
  other arithmetic  66.1 us (5%)
  blocking collectives  42.7 us (3%)
  local copies, waits for them, and re-layouts  27.7 us (2%)
  between operations  15.3 us (1%)
    psum x2, waiting for transfers between devices, _expand_plane(): local_values = lax.psum(local_values, s)  640 us
    ppermute x3, starting transfers between devices, from_partner(): lax.ppermute(value, axis, [(i, i ^ 1 << distance) for i in range(lax.axis...  153 us
    ppermute x18, waiting for transfers between devices, with_halo(): lax.ppermute(tail, axis, [(i, (i + 1) % count) for i in range(ends)])  129 us
    ppermute x18, starting transfers between devices, with_halo(): lax.ppermute(tail, axis, [(i, (i + 1) % count) for i in range(ends)])  108 us
    ppermute x18, waiting for transfers between devices, with_halo(): lax.ppermute(head, axis, [((i + 1) % count, i) for i in range(ends)])  86.5 us
    concatenate x13, other arithmetic, with_halo(): jnp.concatenate([lax.ppermute(tail, axis, [(i, (i + 1) % count) for i in...  48.8 us
    ppermute x3, waiting for transfers between devices, from_partner(): lax.ppermute(value, axis, [(i, i ^ 1 << distance) for i in range(lax.axis...  44 us
    all_to_all x3, blocking collectives, local(): lax.all_to_all(message, 'cols', split_axis=0, concat_axis=2, tiled=True)  42.7 us
  transfers between devices with their start and end apart: 41, of which 38 were waited for; matrix products, arithmetic and copies ran while one was open for 2% of the time, Pallas kernels for 0%

profile of v1, /device:TPU:1, one launch (start us, length us, event | category | flops | bytes accessed | tf_op | source)
XLA Modules:
  0.0 1359.7 jit_solution(5489160827162097863)
XLA Ops:
  27.6 6.9 conditional.14
  34.7 20.1 %all_to_all.45 = bf16[4,6,24,728]{3,2,1,0:T(8,128)(2,1)S(1)} all-to-all(bf16[4,6,24,728]{3,2,1,0:T(8,128)(2,1)S(1)} %copy.117), channel_id=1, replica_groups=mesh['section'=2,'rows'=16,'cols'=4] {'cols'}, dimensions={0} | all-to-all | bytes 1677312 | tf_op jit(solution)/shard_map/all_to_all | solution.py:276
  55.0 22.2 %collective-permute-done.4 = bf16[6,96,728]{2,1,0:T(8,128)(2,1)S(1)} collective-permute-done((bf16[6,96,728]{2,1,0:T(8,128)(2,1)S(1)}, bf16[6,96,728]{2,1,0:T(8,128)(2,1)S(1)}, u32[]{:S(2)}, u32[]{:S(2)}) %collective-permute-start.4) | collective-permute-done | bytes 838688 | tf_op jit(solution)/shard_map/ppermute | solution.py:43
  88.6 8.5 collective-permute-done.6
  102.0 9.4 collective-permute-done.7
  115.3 8.9 pad_maximum_fusion.4
  125.1 13.4 collective-permute-start.9
  150.3 11.5 collective-permute-done.11
  180.2 9.5 collective-permute-done.14
  195.4 21.6 %collective-permute-done.15 = bf16[66,21,512]{2,0,1:T(8,128)(2,1)S(1)} collective-permute-done((bf16[66,21,512]{2,0,1:T(8,128)(2,1)S(1)}, bf16[66,21,512]{2,0,1:T(8,128)(2,1)S(1)}, u32[]{:S(2)}, u32[]{:S(2)}) %collective-permute-start.15) | collective-permute-done | bytes 1419296 | tf_op jit(solution)/shard_map/ppermute | solution.py:33
  227.7 12.3 collective-permute-start.17
  247.2 8.5 collective-permute-done.18
  276.0 6.0 pad_maximum_fusion.5
  283.7 11.3 all_to_all.46
  295.0 77.3 %collective-permute-start.21 = (bf16[6,96,728]{2,1,0:T(8,128)(2,1)S(1)}, bf16[6,96,728]{2,1,0:T(8,128)(2,1)}, u32[]{:S(2)}, u32[]{:S(2)}) collective-permute-start(bf16[6,96,728]{2,1,0:T(8,128)(2,1)S(1)} %bitcast.368), channel_id=1, source_target_pairs={{0,64},{64,0},{1,65},{65,1},{2,66},{66,2},{3,67},{67,3},{4,68},{68... | collective-permute-start | bytes 2515976 | tf_op jit(solution)/shard_map/ppermute | solution.py:43
  372.2 11.3 collective-permute-done.21
  384.0 21.8 %collective-permute-start.22 = (bf16[6,24,2048]{2,1,0:T(8,128)(2,1)S(1)}, bf16[6,24,2048]{2,1,0:T(8,128)(2,1)S(1)}, u32[]{:S(2)}, u32[]{:S(2)}) collective-permute-start(bf16[6,24,2048]{2,1,0:T(8,128)(2,1)S(1)} %get-tuple-element.628), channel_id=1, source_target_pairs={{0,4},{4,8},{8,12},{12,16},{16,20},{20,24},{24,28},{28,32},{32,36}... | collective-permute-start | bytes 1769480 | tf_op jit(solution)/shard_map/ppermute | solution.py:33
  421.9 13.1 collective-permute-done.24
  439.1 8.9 pad_maximum_fusion.6
  449.1 7.4 collective-permute-start.26
  460.1 6.9 collective-permute-done.27
  471.0 9.2 collective-permute-done.28
  486.8 8.7 collective-permute-start.30
  512.2 25.2 %collective-permute-done.32 = bf16[66,21,512]{2,0,1:T(8,128)(2,1)S(1)} collective-permute-done((bf16[66,21,512]{2,0,1:T(8,128)(2,1)S(1)}, bf16[66,21,512]{2,0,1:T(8,128)(2,1)S(1)}, u32[]{:S(2)}, u32[]{:S(2)}) %collective-permute-start.32) | collective-permute-done | bytes 1419296 | tf_op jit(solution)/shard_map/ppermute | solution.py:33
  548.2 8.3 collective-permute-start.34
  573.3 12.3 collective-permute-done.36
  589.8 8.9 pad_maximum_fusion.7
  599.1 11.3 all_to_all.47
  610.4 75.9 %collective-permute-start.38 = (bf16[6,96,728]{2,1,0:T(8,128)(2,1)S(1)}, bf16[6,96,728]{2,1,0:T(8,128)(2,1)}, u32[]{:S(2)}, u32[]{:S(2)}) collective-permute-start(bf16[6,96,728]{2,1,0:T(8,128)(2,1)S(1)} %bitcast.363), channel_id=1, source_target_pairs={{0,64},{64,0},{1,65},{65,1},{2,66},{66,2},{3,67},{67,3},{4,68},{68... | collective-permute-start | bytes 2515976 | tf_op jit(solution)/shard_map/ppermute | solution.py:43
  690.9 10.4 collective-permute-done.38
  708.6 555.7 %all-reduce.7.cloned.1.call-done = (f32[728,728]{1,0:T(8,128)}, f32[2,256,256]{2,1,0:T(8,128)}) async-done(((f32[728,728]{1,0:T(8,128)}, f32[2,256,256]{2,1,0:T(8,128)}), (f32[728,728]{1,0:T(8,128)}, f32[2,256,256]{2,1,0:T(8,128)})) %all-reduce.7.cloned.1.call-update) | async-done | bytes 2644240 | tf_op jit(solution)/shard_map/psum | solution.py:14
  1264.3 84.2 %all-reduce.9.cloned.1.call-done = (f32[728,728]{1,0:T(8,128)}, f32[2,256,256]{2,1,0:T(8,128)}) async-done(((f32[728,728]{1,0:T(8,128)}, f32[2,256,256]{2,1,0:T(8,128)}), (f32[728,728]{1,0:T(8,128)}, f32[2,256,256]{2,1,0:T(8,128)})) %all-reduce.9.cloned.1.call-update) | async-done | bytes 2644240 | tf_op jit(solution)/shard_map/psum | solution.py:14
  (197 shorter events, 242.4 us)
Async XLA Ops:
  7.2 1257.1 %all-reduce.7.cloned.1.call-start = ((), (), s32[]{:S(2)}) async-start(), calls=%async_computation.3 | async-start | bytes 5521408 | tf_op jit(solution)/shard_map/psum | solution.py:14
  8.4 17.4 %collective-permute-start.2 = (bf16[1,96,728]{2,1,0:T(8,128)(2,1)S(1)}, bf16[1,96,728]{2,1,0:T(8,128)(2,1)S(1)}, u32[]{:S(2)}, u32[]{:S(2)}) collective-permute-start(bf16[1,96,728]{2,1,0:T(8,128)(2,1)S(1)} %get-tuple-element.638), channel_id=1, source_target_pairs={{0,1},{1,2},{2,3},{3,4},{4,5},{5,6},{6,7},{7,8},{8,9},{9,10},{10,1... | collective-permute-start | bytes 419336 | tf_op jit(solution)/shard_map/ppermute | solution.py:33
  12.8 13.0 collective-permute-start.1
  54.9 22.3 %collective-permute-start.4 = (bf16[6,96,728]{2,1,0:T(8,128)(2,1)S(1)}, bf16[6,96,728]{2,1,0:T(8,128)(2,1)S(1)}, u32[]{:S(2)}, u32[]{:S(2)}) collective-permute-start(bf16[6,96,728]{2,1,0:T(8,128)(2,1)S(1)} %bitcast.367), channel_id=1, source_target_pairs={{0,64},{64,0},{1,65},{65,1},{2,66},{66,2},{3,67},{67,3},{4,68},{68... | collective-permute-start | bytes 2515976 | tf_op jit(solution)/shard_map/ppermute | solution.py:43
  81.4 15.7 %collective-permute-start.6 = (bf16[6,24,2048]{2,1,0:T(8,128)(2,1)S(1)}, bf16[6,24,2048]{2,1,0:T(8,128)(2,1)S(1)}, u32[]{:S(2)}, u32[]{:S(2)}) collective-permute-start(bf16[6,24,2048]{2,1,0:T(8,128)(2,1)S(1)} %get-tuple-element.633), channel_id=1, source_target_pairs={{4,0},{8,4},{12,8},{16,12},{20,16},{24,20},{28,24},{32,28},{36,32}... | collective-permute-start | bytes 1769480 | tf_op jit(solution)/shard_map/ppermute | solution.py:35
  98.2 13.2 collective-permute-start.7
  100.5 14.8 %collective-permute-start.8 = (bf16[36,6,2048]{2,0,1:T(8,128)(2,1)S(1)}, bf16[36,6,2048]{2,0,1:T(8,128)(2,1)S(1)}, u32[]{:S(2)}, u32[]{:S(2)}) collective-permute-start(bf16[36,6,2048]{2,0,1:T(8,128)(2,1)S(1)} %get-tuple-element.625), channel_id=1, source_target_pairs={{1,0},{2,1},{3,2},{5,4},{6,5},{7,6},{9,8},{10,9},{11,10},{13,12},{... | collective-permute-start | bytes 2654216 | tf_op jit(solution)/shard_map/ppermute | solution.py:35
  125.1 17.0 %collective-permute-start.9 = (bf16[21,24,256]{2,0,1:T(8,128)(2,1)S(1)}, bf16[21,24,256]{2,0,1:T(8,128)(2,1)S(1)}, u32[]{:S(2)}, u32[]{:S(2)}) collective-permute-start(bf16[21,24,256]{2,0,1:T(8,128)(2,1)S(1)} %get-tuple-element.654), channel_id=1, source_target_pairs={{0,4},{4,8},{8,12},{12,16},{16,20},{20,24},{24,28},{28,32},{32,36}... | collective-permute-start | bytes 774152 | tf_op jit(solution)/shard_map/ppermute | solution.py:33
  147.4 14.4 %collective-permute-start.11 = (bf16[66,21,256]{2,0,1:T(8,128)(2,1)S(1)}, bf16[66,21,256]{2,0,1:T(8,128)(2,1)S(1)}, u32[]{:S(2)}, u32[]{:S(2)}) collective-permute-start(bf16[66,21,256]{2,0,1:T(8,128)(2,1)S(1)} %get-tuple-element.646), channel_id=1, source_target_pairs={{0,1},{1,2},{2,3},{4,5},{5,6},{6,7},{8,9},{9,10},{10,11},{12,13},{... | collective-permute-start | bytes 2128904 | tf_op jit(solution)/shard_map/ppermute | solution.py:33
  149.0 17.1 %collective-permute-start.12 = (bf16[66,21,256]{2,0,1:T(8,128)(2,1)S(1)}, bf16[66,21,256]{2,0,1:T(8,128)(2,1)S(1)}, u32[]{:S(2)}, u32[]{:S(2)}) collective-permute-start(bf16[66,21,256]{2,0,1:T(8,128)(2,1)S(1)} %get-tuple-element.647), channel_id=1, source_target_pairs={{1,0},{2,1},{3,2},{5,4},{6,5},{7,6},{9,8},{10,9},{11,10},{13,12},{... | collective-permute-start | bytes 2128904 | tf_op jit(solution)/shard_map/ppermute | solution.py:35
  174.0 15.6 %collective-permute-start.14 = (bf16[21,24,512]{2,1,0:T(8,128)(2,1)S(1)}, bf16[21,24,512]{2,1,0:T(8,128)(2,1)S(1)}, u32[]{:S(2)}, u32[]{:S(2)}) collective-permute-start(bf16[21,24,512]{2,1,0:T(8,128)(2,1)S(1)} %get-tuple-element.651), channel_id=1, source_target_pairs={{4,0},{8,4},{12,8},{16,12},{20,16},{24,20},{28,24},{32,28},{36,32}... | collective-permute-start | bytes 1548296 | tf_op jit(solution)/shard_map/ppermute | solution.py:35
  190.7 26.3 %collective-permute-start.15 = (bf16[66,21,512]{2,0,1:T(8,128)(2,1)S(1)}, bf16[66,21,512]{2,0,1:T(8,128)(2,1)S(1)}, u32[]{:S(2)}, u32[]{:S(2)}) collective-permute-start(bf16[66,21,512]{2,0,1:T(8,128)(2,1)S(1)} %get-tuple-element.636), channel_id=1, source_target_pairs={{0,1},{1,2},{2,3},{4,5},{5,6},{6,7},{8,9},{9,10},{10,11},{12,13},{... | collective-permute-start | bytes 4257800 | tf_op jit(solution)/shard_map/ppermute | solution.py:33
  194.1 27.1 %collective-permute-start.16 = (bf16[66,21,512]{2,0,1:T(8,128)(2,1)S(1)}, bf16[66,21,512]{2,0,1:T(8,128)(2,1)S(1)}, u32[]{:S(2)}, u32[]{:S(2)}) collective-permute-start(bf16[66,21,512]{2,0,1:T(8,128)(2,1)S(1)} %get-tuple-element.637), channel_id=1, source_target_pairs={{1,0},{2,1},{3,2},{5,4},{6,5},{7,6},{9,8},{10,9},{11,10},{13,12},{... | collective-permute-start | bytes 4257800 | tf_op jit(solution)/shard_map/ppermute | solution.py:35
  227.7 19.1 %collective-permute-start.17 = (bf16[6,24,2048]{2,1,0:T(8,128)(2,1)S(1)}, bf16[6,24,2048]{2,1,0:T(8,128)(2,1)S(1)}, u32[]{:S(2)}, u32[]{:S(2)}) collective-permute-start(bf16[6,24,2048]{2,1,0:T(8,128)(2,1)S(1)} %get-tuple-element.630), channel_id=1, source_target_pairs={{0,4},{4,8},{8,12},{12,16},{16,20},{20,24},{24,28},{28,32},{32,36}... | collective-permute-start | bytes 1769480 | tf_op jit(solution)/shard_map/ppermute | solution.py:33
  240.1 15.6 %collective-permute-start.18 = (bf16[6,24,2048]{2,1,0:T(8,128)(2,1)S(1)}, bf16[6,24,2048]{2,1,0:T(8,128)(2,1)S(1)}, u32[]{:S(2)}, u32[]{:S(2)}) collective-permute-start(bf16[6,24,2048]{2,1,0:T(8,128)(2,1)S(1)} %get-tuple-element.631), channel_id=1, source_target_pairs={{4,0},{8,4},{12,8},{16,12},{20,16},{24,20},{28,24},{32,28},{36,32}... | collective-permute-start | bytes 1769480 | tf_op jit(solution)/shard_map/ppermute | solution.py:35
  258.1 13.2 collective-permute-start.19
  260.9 15.1 %collective-permute-start.20 = (bf16[36,6,2048]{2,0,1:T(8,128)(2,1)}, bf16[36,6,2048]{2,0,1:T(8,128)(2,1)}, u32[]{:S(2)}, u32[]{:S(2)}) collective-permute-start(bf16[36,6,2048]{2,0,1:T(8,128)(2,1)} %get-tuple-element.623), channel_id=1, source_target_pairs={{1,0},{2,1},{3,2},{5,4},{6,5},{7,6},{9,8},{10,9},{11,10},{13,12},{... | collective-permute-start | bytes 2654216 | tf_op jit(solution)/shard_map/ppermute | solution.py:35
  295.0 88.6 %collective-permute-start.21 = (bf16[6,96,728]{2,1,0:T(8,128)(2,1)S(1)}, bf16[6,96,728]{2,1,0:T(8,128)(2,1)}, u32[]{:S(2)}, u32[]{:S(2)}) collective-permute-start(bf16[6,96,728]{2,1,0:T(8,128)(2,1)S(1)} %bitcast.368), channel_id=1, source_target_pairs={{0,64},{64,0},{1,65},{65,1},{2,66},{66,2},{3,67},{67,3},{4,68},{68... | collective-permute-start | bytes 2515976 | tf_op jit(solution)/shard_map/ppermute | solution.py:43
  384.0 28.6 %collective-permute-start.22 = (bf16[6,24,2048]{2,1,0:T(8,128)(2,1)S(1)}, bf16[6,24,2048]{2,1,0:T(8,128)(2,1)S(1)}, u32[]{:S(2)}, u32[]{:S(2)}) collective-permute-start(bf16[6,24,2048]{2,1,0:T(8,128)(2,1)S(1)} %get-tuple-element.628), channel_id=1, source_target_pairs={{0,4},{4,8},{8,12},{12,16},{16,20},{20,24},{24,28},{28,32},{32,36}... | collective-permute-start | bytes 1769480 | tf_op jit(solution)/shard_map/ppermute | solution.py:33
  418.0 16.9 %collective-permute-start.24 = (bf16[36,6,2048]{2,0,1:T(8,128)(2,1)S(1)}, bf16[36,6,2048]{2,0,1:T(8,128)(2,1)S(1)}, u32[]{:S(2)}, u32[]{:S(2)}) collective-permute-start(bf16[36,6,2048]{2,0,1:T(8,128)(2,1)S(1)} %get-tuple-element.620), channel_id=1, source_target_pairs={{0,1},{1,2},{2,3},{4,5},{5,6},{6,7},{8,9},{9,10},{10,11},{12,13},{... | collective-permute-start | bytes 2654216 | tf_op jit(solution)/shard_map/ppermute | solution.py:33
  420.6 18.5 %collective-permute-start.25 = (bf16[36,6,2048]{2,0,1:T(8,128)(2,1)S(1)}, bf16[36,6,2048]{2,0,1:T(8,128)(2,1)S(1)}, u32[]{:S(2)}, u32[]{:S(2)}) collective-permute-start(bf16[36,6,2048]{2,0,1:T(8,128)(2,1)S(1)} %get-tuple-element.621), channel_id=1, source_target_pairs={{1,0},{2,1},{3,2},{5,4},{6,5},{7,6},{9,8},{10,9},{11,10},{13,12},{... | collective-permute-start | bytes 2654216 | tf_op jit(solution)/shard_map/ppermute | solution.py:35
  467.5 12.7 collective-permute-start.28
  469.7 14.7 %collective-permute-start.29 = (bf16[66,21,256]{2,0,1:T(8,128)(2,1)S(1)}, bf16[66,21,256]{2,0,1:T(8,128)(2,1)S(1)}, u32[]{:S(2)}, u32[]{:S(2)}) collective-permute-start(bf16[66,21,256]{2,0,1:T(8,128)(2,1)S(1)} %get-tuple-element.645), channel_id=1, source_target_pairs={{1,0},{2,1},{3,2},{5,4},{6,5},{7,6},{9,8},{10,9},{11,10},{13,12},{... | collective-permute-start | bytes 2128904 | tf_op jit(solution)/shard_map/ppermute | solution.py:35
  486.8 14.7 %collective-permute-start.30 = (bf16[21,24,512]{2,1,0:T(8,128)(2,1)S(1)}, bf16[21,24,512]{2,1,0:T(8,128)(2,1)S(1)}, u32[]{:S(2)}, u32[]{:S(2)}) collective-permute-start(bf16[21,24,512]{2,1,0:T(8,128)(2,1)S(1)} %get-tuple-element.648), channel_id=1, source_target_pairs={{0,4},{4,8},{8,12},{12,16},{16,20},{20,24},{24,28},{28,32},{32,36}... | collective-permute-start | bytes 1548296 | tf_op jit(solution)/shard_map/ppermute | solution.py:33
  507.7 29.7 %collective-permute-start.32 = (bf16[66,21,512]{2,0,1:T(8,128)(2,1)S(1)}, bf16[66,21,512]{2,0,1:T(8,128)(2,1)S(1)}, u32[]{:S(2)}, u32[]{:S(2)}) collective-permute-start(bf16[66,21,512]{2,0,1:T(8,128)(2,1)S(1)} %get-tuple-element.634), channel_id=1, source_target_pairs={{0,1},{1,2},{2,3},{4,5},{5,6},{6,7},{8,9},{9,10},{10,11},{12,13},{... | collective-permute-start | bytes 4257800 | tf_op jit(solution)/shard_map/ppermute | solution.py:33
  510.9 30.7 %collective-permute-start.33 = (bf16[66,21,512]{2,0,1:T(8,128)(2,1)S(1)}, bf16[66,21,512]{2,0,1:T(8,128)(2,1)S(1)}, u32[]{:S(2)}, u32[]{:S(2)}) collective-permute-start(bf16[66,21,512]{2,0,1:T(8,128)(2,1)S(1)} %get-tuple-element.635), channel_id=1, source_target_pairs={{1,0},{2,1},{3,2},{5,4},{6,5},{7,6},{9,8},{10,9},{11,10},{13,12},{... | collective-permute-start | bytes 4257800 | tf_op jit(solution)/shard_map/ppermute | solution.py:35
  548.2 15.1 %collective-permute-start.34 = (bf16[6,24,2048]{2,1,0:T(8,128)(2,1)S(1)}, bf16[6,24,2048]{2,1,0:T(8,128)(2,1)S(1)}, u32[]{:S(2)}, u32[]{:S(2)}) collective-permute-start(bf16[6,24,2048]{2,1,0:T(8,128)(2,1)S(1)} %get-tuple-element.626), channel_id=1, source_target_pairs={{0,4},{4,8},{8,12},{12,16},{16,20},{20,24},{24,28},{28,32},{32,36}... | collective-permute-start | bytes 1769480 | tf_op jit(solution)/shard_map/ppermute | solution.py:33
  556.5 11.9 collective-permute-start.35
  569.5 16.1 %collective-permute-start.36 = (bf16[36,6,2048]{2,0,1:T(8,128)(2,1)S(1)}, bf16[36,6,2048]{2,0,1:T(8,128)(2,1)S(1)}, u32[]{:S(2)}, u32[]{:S(2)}) collective-permute-start(bf16[36,6,2048]{2,0,1:T(8,128)(2,1)S(1)} %get-tuple-element.618), channel_id=1, source_target_pairs={{0,1},{1,2},{2,3},{4,5},{5,6},{6,7},{8,9},{9,10},{10,11},{12,13},{... | collective-permute-start | bytes 2654216 | tf_op jit(solution)/shard_map/ppermute | solution.py:33
  572.0 17.8 %collective-permute-start.37 = (bf16[36,6,2048]{2,0,1:T(8,128)(2,1)S(1)}, bf16[36,6,2048]{2,0,1:T(8,128)(2,1)S(1)}, u32[]{:S(2)}, u32[]{:S(2)}) collective-permute-start(bf16[36,6,2048]{2,0,1:T(8,128)(2,1)S(1)} %get-tuple-element.619), channel_id=1, source_target_pairs={{1,0},{2,1},{3,2},{5,4},{6,5},{7,6},{9,8},{10,9},{11,10},{13,12},{... | collective-permute-start | bytes 2654216 | tf_op jit(solution)/shard_map/ppermute | solution.py:35
  610.4 90.9 %collective-permute-start.38 = (bf16[6,96,728]{2,1,0:T(8,128)(2,1)S(1)}, bf16[6,96,728]{2,1,0:T(8,128)(2,1)}, u32[]{:S(2)}, u32[]{:S(2)}) collective-permute-start(bf16[6,96,728]{2,1,0:T(8,128)(2,1)S(1)} %bitcast.363), channel_id=1, source_target_pairs={{0,64},{64,0},{1,65},{65,1},{2,66},{66,2},{3,67},{67,3},{4,68},{68... | collective-permute-start | bytes 2515976 | tf_op jit(solution)/shard_map/ppermute | solution.py:43
  708.5 640.0 %all-reduce.9.cloned.1.call-start = ((), (), s32[]{:S(2)}) async-start(), calls=%async_computation.4 | async-start | bytes 5521408 | tf_op jit(solution)/shard_map/psum | solution.py:14
  (28 other events, 297.7 us)
Sparse Core Ops, SparseCore 0:
  708.6 555.5 all-reduce.6
  1266.8 81.7 all-reduce.8
